TPU v7x, 512 devices: a whole 4x8x8 slice. The times are simulated.
512 devices in a mesh: dp: 64 (over x, y, core), code: 8 (over z).
Axes of the slice: x: 4, y: 8, z: 8, core: 2. Of those that a mesh axis runs over, the one named last changes fastest.
Arguments:
- items: float32 [65536, 512], P(('dp', 'code')), may hold values from -6 to 6
- codewords: float32 [8192, 512], P('code'), may hold values from -6 to 6
- assign: int32 [65536], P('dp'), may hold values from 0 to 8191, as said below
Outputs:
- new_codewords: float32 [8192, 512], P('code', 'dp')
- residual: float32 [65536, 512], P(('dp', 'code'))
Inputs may be any that keep to these rules, and one draw needn't show every extreme that they name: `assign`: the items are laid out in aligned blocks of 128 (the items of one device). Splitting the codewords into equal ranges, one per index of code, the items of one block name codewords of exactly half of the ranges, 32 items for each such range.
All inputs are finite; a program needn't handle non-finite values.
Results may differ from a plain program's by a relative error of at most 0.0003.
Values sent between devices are 32-bit elements; how exact they have to be, the bound alone decides.
No kernel may reach another device: no remote copies, remote signals or barrier semaphores. Data moves between devices by JAX's collectives and lax.ppermute only.
A program may use at most 64 MiB of HBM per device.

v0:
```python
import jax
import jax.numpy as jnp
from jax import lax
from jax.sharding import Mesh, PartitionSpec as P

K = 8192
ITERS = 3
DP = ("x", "y", "core")
epsilon = 1e-05
inverse_temp = 64.0


def unit_rows(values):
    return values * lax.rsqrt(jnp.mean(values * values, axis=-1, keepdims=True) + epsilon)


def exchange_sum(part, axes):
    count = lax.axis_size(axes)
    copies = jnp.broadcast_to(part[None], (count,) + part.shape)
    return jnp.sum(lax.all_to_all(copies, axes, 0, 0), axis=0)


def scatter_sum(blocks, axis):
    return jnp.sum(lax.all_to_all(blocks, axis, 0, 0), axis=0)


def body(items, codewords, assign):
    code_count = lax.axis_size("code")
    dp_count = lax.axis_size(DP)
    local_codes = codewords.shape[0]
    own_rows, width = items.shape
    total_items = own_rows * code_count * dp_count
    scaled = unit_rows(codewords) * (inverse_temp / width)
    gathered = lax.all_gather(items, "code", axis=0, tiled=True)
    logits = lax.dot_general(
        unit_rows(gathered),
        scaled,
        (((1,), (1,)), ((), ())),
        precision=lax.Precision.HIGH,
        preferred_element_type=jnp.float32,
    )
    kernel_vals = jnp.exp(logits)
    col_part = jnp.sum(kernel_vals, axis=0)
    for _ in range(ITERS):
        col_scale = 1.0 / (K * exchange_sum(col_part, DP))
        row_part = jnp.sum(kernel_vals * col_scale[None, :], axis=1)
        row_scale = 1.0 / (total_items * exchange_sum(row_part, "code"))
        col_part = jnp.sum(kernel_vals * row_scale[:, None], axis=0)
    mass = exchange_sum(col_part, DP)
    nx, ny, nc = (lax.axis_size("x"), lax.axis_size("y"), lax.axis_size("core"))
    cols = width // dp_count
    numerator = lax.dot_general(
        row_scale[:, None] * gathered,
        kernel_vals,
        (((0,), (0,)), ((), ())),
        precision=lax.Precision.HIGH,
        preferred_element_type=jnp.float32,
    )
    halves = numerator.reshape(nx * ny, nc, cols, local_codes)
    core = lax.axis_index("core")
    mine = lax.dynamic_index_in_dim(halves, core, 1, keepdims=False)
    other = lax.dynamic_index_in_dim(halves, 1 - core, 1, keepdims=False)
    chip = mine + lax.ppermute(other, "core", [(0, 1), (1, 0)])
    owned = scatter_sum(chip.reshape(nx, ny, cols, local_codes), "x")
    owned = scatter_sum(owned, "y")
    new_codewords = (owned / mass[None, :]).T
    my_code = lax.axis_index("code")
    offset = my_code * local_codes
    index_rows = assign - offset
    inside = (index_rows >= 0) & (index_rows < local_codes)
    picked = jnp.take(codewords, jnp.clip(index_rows, 0, local_codes - 1), axis=0)
    looked = lax.psum_scatter(
        jnp.where(inside[:, None], picked, jnp.float32(0.0)),
        "code",
        scatter_dimension=0,
        tiled=True,
    )
    residual = items - looked
    return (new_codewords, residual)


def solution(mesh):
    cores = 2
    ny = 8
    dp, code = mesh.devices.shape
    fine = Mesh(
        mesh.devices.reshape(dp // (ny * cores), ny, cores, code), ("x", "y", "core", "code")
    )
    in_specs = (P(DP + ("code",), None), P("code", None), P(DP))
    out_specs = (P("code", DP), P(DP + ("code",), None))
    return jax.shard_map(body, mesh=fine, in_specs=in_specs, out_specs=out_specs, check_vma=False)
```

profile of v0, /device:TPU:1, one launch (start us, length us, event | category | flops | bytes accessed | tf_op | source)
XLA Modules:
  0.0 254.8 jit_solution(13360606303036772084)
XLA Ops:
  7.2 0.7 all-gather.2.cloned.1.call-update
  7.9 2.0 multiply_reduce_fusion.6
  9.9 46.3 %all-gather.2.cloned.1.call-done = f32[1024,512]{1,0:T(8,128)} async-done(((f32[128,512]{1,0:T(8,128)}), f32[1024,512]{1,0:T(8,128)}) %all-gather.2.cloned.1.call-update) | async-done | bytes 2097168 | tf_op jit(solution)/shard_map/all_gather | solution.py:34
  56.2 2.0 multiply_reduce_fusion.7
  58.2 0.2 copy-done.1
  58.4 5.6 %exponential_reduce_fusion = (f32[1024]{0:T(1024)S(1)}, f32[1024,1024]{1,0:T(8,128)}) fusion(f32[1024,512]{1,0:T(8,128)S(1)} %copy-done, f32[1024]{0:T(1024)S(1)} %add_rsqrt_fusion, f32[1024,512]{1,0:T(8,128)S(1)} %copy-done.1, f32[1024]{0:T(1024)S(1)} %add_rsqrt_fusion.1), kind=kOutput, calls=%fused_computation.9 | convolution fusion | flops 3223845888 | bytes 8400896 | tf_op jit(solution)/shard_map/dot_general | solution.py:35
  64.0 0.1 broadcast_in_dim.31
  64.1 26.2 %all_to_all.52 = f32[64,1,1024]{2,1,0:T(1,128)S(1)} all-to-all(f32[64,1,1024]{2,1,0:T(1,128)S(1)} %broadcast_in_dim.31), channel_id=1, replica_groups=mesh['x'=4,'y'=8,'core'=2,'code'=8] {'x','y','core'}, dimensions={0} | all-to-all | bytes 524288 | tf_op jit(solution)/shard_map/all_to_all | solution.py:20
  90.4 0.2 reduce_sum.165
  90.5 2.9 %multiply_reduce_fusion.5 = f32[1024]{0:T(1024)S(1)} fusion(f32[1024,1024]{1,0:T(8,128)} %get-tuple-element.5, f32[1024]{0:T(1024)S(1)} %multiply_divide_fusion.5), kind=kLoop, calls=%fused_computation.6 | loop fusion | flops 2096128 | bytes 4202496 | tf_op jit(solution)/shard_map/reduce_sum | solution.py:46
  93.4 10.5 %all_to_all.53 = f32[8,1,1024]{2,1,0:T(1,128)S(1)} all-to-all(f32[8,1,1024]{2,1,0:T(1,128)S(1)} %broadcast_in_dim.32), channel_id=1, replica_groups=mesh['x'=4,'y'=8,'core'=2,'code'=8] {'code'}, dimensions={0} | all-to-all | bytes 65536 | tf_op jit(solution)/shard_map/all_to_all | solution.py:20
  104.0 2.8 %multiply_reduce_fusion.4 = f32[1024]{0:T(1024)S(1)} fusion(f32[1024,1024]{1,0:T(8,128)} %get-tuple-element.5, f32[1024]{0:T(1024)S(1)} %multiply_divide_fusion.4), kind=kLoop, calls=%fused_computation.5 | loop fusion | flops 2096128 | bytes 4202496 | tf_op jit(solution)/shard_map/reduce_sum | solution.py:48
  106.8 0.8 broadcast_in_dim.33
  107.7 7.5 %all-to-all-start.2 = ((f32[64,1,1024]{2,1,0:T(1,128)}), f32[64,1,1024]{2,1,0:T(1,128)S(1)}, u32[]{:S(2)}, u32[]{:S(2)}) async-start(f32[64,1,1024]{2,1,0:T(1,128)} %broadcast_in_dim.33), calls=%async_computation.2 | async-start | bytes 524288 | tf_op jit(solution)/shard_map/all_to_all | solution.py:20
  115.1 12.0 %all-to-all-done.2 = f32[64,1,1024]{2,1,0:T(1,128)S(1)} async-done(((f32[64,1,1024]{2,1,0:T(1,128)}), f32[64,1,1024]{2,1,0:T(1,128)S(1)}, u32[]{:S(2)}, u32[]{:S(2)}) %all-to-all-start.2) | async-done | bytes 262176 | tf_op jit(solution)/shard_map/all_to_all | solution.py:20
  127.1 0.2 reduce_sum.169
  127.3 2.9 %multiply_reduce_fusion.3 = f32[1024]{0:T(1024)S(1)} fusion(f32[1024,1024]{1,0:T(8,128)} %get-tuple-element.5, f32[1024]{0:T(1024)S(1)} %multiply_divide_fusion.3), kind=kLoop, calls=%fused_computation.4 | loop fusion | flops 2096128 | bytes 4202496 | tf_op jit(solution)/shard_map/reduce_sum | solution.py:46
  130.2 0.6 broadcast_in_dim.34
  130.8 3.3 %all-to-all-start.3 = ((f32[8,1,1024]{2,1,0:T(1,128)}), f32[8,1,1024]{2,1,0:T(1,128)S(1)}, u32[]{:S(2)}, u32[]{:S(2)}) async-start(f32[8,1,1024]{2,1,0:T(1,128)} %broadcast_in_dim.34), calls=%async_computation.3 | async-start | bytes 65536 | tf_op jit(solution)/shard_map/all_to_all | solution.py:20
  134.2 4.9 %gather_fusion = f32[1024,512]{1,0:T(8,128)} fusion(f32[1024,512]{1,0:T(8,128)S(1)} %copy-done, s32[1024]{0:T(1024)S(1)} %fusion.11), kind=kCustom, calls=%fused_computation | custom fusion | bytes 4198400 | tf_op jit(solution)/shard_map/jit(_take)/gather | solution.py:71
  139.1 1.9 all-to-all-done.3
  141.0 2.9 %multiply_reduce_fusion.2 = f32[1024]{0:T(1024)S(1)} fusion(f32[1024,1024]{1,0:T(8,128)} %get-tuple-element.5, f32[1024]{0:T(1024)S(1)} %multiply_divide_fusion.2), kind=kLoop, calls=%fused_computation.3 | loop fusion | flops 2096128 | bytes 4202496 | tf_op jit(solution)/shard_map/reduce_sum | solution.py:48
  144.0 0.8 broadcast_in_dim.35
  144.8 7.2 %all-to-all-start.4 = ((f32[64,1,1024]{2,1,0:T(1,128)}), f32[64,1,1024]{2,1,0:T(1,128)S(1)}, u32[]{:S(2)}, u32[]{:S(2)}) async-start(f32[64,1,1024]{2,1,0:T(1,128)} %broadcast_in_dim.35), calls=%async_computation.4 | async-start | bytes 524288 | tf_op jit(solution)/shard_map/all_to_all | solution.py:20
  152.1 2.0 select_select_fusion
  154.1 9.9 %all-to-all-done.4 = f32[64,1,1024]{2,1,0:T(1,128)S(1)} async-done(((f32[64,1,1024]{2,1,0:T(1,128)}), f32[64,1,1024]{2,1,0:T(1,128)S(1)}, u32[]{:S(2)}, u32[]{:S(2)}) %all-to-all-start.4) | async-done | bytes 262176 | tf_op jit(solution)/shard_map/all_to_all | solution.py:20
  164.0 0.2 reduce_sum.173
  164.2 3.0 %multiply_reduce_fusion.1 = f32[1024]{0:T(1024)S(1)} fusion(f32[1024,1024]{1,0:T(8,128)} %get-tuple-element.5, f32[1024]{0:T(1024)S(1)} %multiply_divide_fusion.1), kind=kLoop, calls=%fused_computation.2 | loop fusion | flops 2096128 | bytes 4202496 | tf_op jit(solution)/shard_map/reduce_sum | solution.py:46
  167.2 0.6 broadcast_in_dim.36
  167.9 3.8 %all-to-all-start.5 = ((f32[8,1,1024]{2,1,0:T(1,128)}), f32[8,1,1024]{2,1,0:T(1,128)S(1)}, u32[]{:S(2)}, u32[]{:S(2)}) async-start(f32[8,1,1024]{2,1,0:T(1,128)} %broadcast_in_dim.36), calls=%async_computation.5 | async-start | bytes 65536 | tf_op jit(solution)/shard_map/all_to_all | solution.py:20
  171.7 7.1 %all-to-all-done.5 = f32[8,1,1024]{2,1,0:T(1,128)S(1)} async-done(((f32[8,1,1024]{2,1,0:T(1,128)}), f32[8,1,1024]{2,1,0:T(1,128)S(1)}, u32[]{:S(2)}, u32[]{:S(2)}) %all-to-all-start.5) | async-done | bytes 32800 | tf_op jit(solution)/shard_map/all_to_all | solution.py:20
  178.9 6.0 %fusion = f32[512,1024]{1,0:T(8,128)S(1)} fusion(f32[1024,1024]{1,0:T(8,128)} %get-tuple-element.5, f32[1024,512]{1,0:T(8,128)S(1)} %copy-done.2, f32[1024]{0:T(1024)S(1)} %multiply_divide_fusion), kind=kOutput, calls=%fused_computation.7 | convolution fusion | flops 3221749760 | bytes 8392704 | tf_op jit(solution)/shard_map/dot_general | solution.py:52
  184.9 1.3 copy-done.4
  186.3 3.8 %collective-permute-start = (f32[32,8,1024]{2,1,0:T(8,128)S(1)}, f32[32,8,1024]{2,1,0:T(8,128)S(1)}, u32[]{:S(2)}, u32[]{:S(2)}) collective-permute-start(f32[32,8,1024]{2,1,0:T(8,128)S(1)} %dynamic-slice_bitcast_fusion), channel_id=1, source_target_pairs={{0,8},{8,0},{1,9},{9,1},{2,10},{10,2},{3,11},{11,3},{4,12},{12,4},... | collective-permute-start | bytes 3145736 | tf_op jit(solution)/shard_map/ppermute | solution.py:63
  190.1 2.3 collective-permute-done
  192.4 2.4 bitcast_add_fusion
  194.8 3.9 %all-to-all-start.6 = ((f32[4,8,8,1024]{3,2,1,0:T(8,128)}), f32[4,8,8,1024]{3,2,1,0:T(8,128)S(1)}, u32[]{:S(2)}, u32[]{:S(2)}) async-start(f32[4,8,8,1024]{3,2,1,0:T(8,128)} %bitcast.3), calls=%async_computation.6 | async-start | bytes 2097152 | tf_op jit(solution)/shard_map/all_to_all | solution.py:24
  198.7 2.8 %multiply_reduce_fusion = f32[1024]{0:T(1024)S(1)} fusion(f32[1024,1024]{1,0:T(8,128)} %get-tuple-element.5, f32[1024]{0:T(1024)S(1)} %multiply_divide_fusion), kind=kLoop, calls=%fused_computation.1 | loop fusion | flops 2096128 | bytes 4202496 | tf_op jit(solution)/shard_map/reduce_sum | solution.py:48
  201.5 11.7 %all-to-all-done.6 = f32[4,8,8,1024]{3,2,1,0:T(8,128)S(1)} async-done(((f32[4,8,8,1024]{3,2,1,0:T(8,128)}), f32[4,8,8,1024]{3,2,1,0:T(8,128)S(1)}, u32[]{:S(2)}, u32[]{:S(2)}) %all-to-all-start.6) | async-done | bytes 1048608 | tf_op jit(solution)/shard_map/all_to_all | solution.py:24
  213.2 0.8 broadcast_in_dim.37
  214.1 6.5 %all-to-all-start.8 = ((f32[64,1,1024]{2,1,0:T(1,128)}), f32[64,1,1024]{2,1,0:T(1,128)S(1)}, u32[]{:S(2)}, u32[]{:S(2)}) async-start(f32[64,1,1024]{2,1,0:T(1,128)} %broadcast_in_dim.37), calls=%async_computation.8 | async-start | bytes 524288 | tf_op jit(solution)/shard_map/all_to_all | solution.py:20
  220.5 0.8 reduce_sum.176
  221.3 11.2 %all-to-all-done.8 = f32[64,1,1024]{2,1,0:T(1,128)S(1)} async-done(((f32[64,1,1024]{2,1,0:T(1,128)}), f32[64,1,1024]{2,1,0:T(1,128)S(1)}, u32[]{:S(2)}, u32[]{:S(2)}) %all-to-all-start.8) | async-done | bytes 262176 | tf_op jit(solution)/shard_map/all_to_all | solution.py:20
  232.5 3.9 %all-to-all-start.7 = ((f32[8,8,1024]{2,1,0:T(8,128)}), f32[8,8,1024]{2,1,0:T(8,128)S(1)}, u32[]{:S(2)}, u32[]{:S(2)}) async-start(f32[8,8,1024]{2,1,0:T(8,128)} %reduce_sum.176), calls=%async_computation.7 | async-start | bytes 524288 | tf_op jit(solution)/shard_map/all_to_all | solution.py:24
  236.4 1.7 sub.15
  238.1 0.2 reduce_sum.179
  238.3 9.0 %all-to-all-done.7 = f32[8,8,1024]{2,1,0:T(8,128)S(1)} async-done(((f32[8,8,1024]{2,1,0:T(8,128)}), f32[8,8,1024]{2,1,0:T(8,128)S(1)}, u32[]{:S(2)}, u32[]{:S(2)}) %all-to-all-start.7) | async-done | bytes 262176 | tf_op jit(solution)/shard_map/all_to_all | solution.py:24
  247.4 0.6 divide_bitcast_fusion
  (32 shorter events, 0.4 us)
Async XLA Ops:
  7.2 49.0 %all-gather.2.cloned.1.call-start = ((), (), s32[]{:S(2)}) async-start(), calls=%async_computation.10 | async-start | bytes 2359296 | tf_op jit(solution)/shard_map/all_gather | solution.py:34
  7.9 50.3 %copy-start = (f32[1024,512]{1,0:T(8,128)S(1)}, f32[1024,512]{1,0:T(8,128)}, u32[]{:S(2)}) copy-start(f32[1024,512]{1,0:T(8,128)} %param.4) | copy-start | bytes 6291460
  56.2 2.2 copy-start.1
  107.7 19.5 %all-to-all-start.2 = ((f32[64,1,1024]{2,1,0:T(1,128)}), f32[64,1,1024]{2,1,0:T(1,128)S(1)}, u32[]{:S(2)}, u32[]{:S(2)}) async-start(f32[64,1,1024]{2,1,0:T(1,128)} %broadcast_in_dim.33), calls=%async_computation.2 | async-start | bytes 524288 | tf_op jit(solution)/shard_map/all_to_all | solution.py:20
  127.3 6.9 %copy-start.6 = (s32[1024]{0:T(1024)S(1)}, s32[1024]{0:T(1024)}, u32[]{:S(2)}) copy-start(s32[1024]{0:T(1024)} %param.5) | copy-start | bytes 12292
  130.8 10.1 %all-to-all-start.3 = ((f32[8,1,1024]{2,1,0:T(1,128)}), f32[8,1,1024]{2,1,0:T(1,128)S(1)}, u32[]{:S(2)}, u32[]{:S(2)}) async-start(f32[8,1,1024]{2,1,0:T(1,128)} %broadcast_in_dim.34), calls=%async_computation.3 | async-start | bytes 65536 | tf_op jit(solution)/shard_map/all_to_all | solution.py:20
  141.0 11.0 %copy-start.3 = (f32[1024,512]{1,0:T(8,128)S(1)}, f32[1024,512]{1,0:T(8,128)}, u32[]{:S(2)}) copy-start(f32[1024,512]{1,0:T(8,128)} %gather_fusion) | copy-start | bytes 6291460
  144.8 19.2 %all-to-all-start.4 = ((f32[64,1,1024]{2,1,0:T(1,128)}), f32[64,1,1024]{2,1,0:T(1,128)S(1)}, u32[]{:S(2)}, u32[]{:S(2)}) async-start(f32[64,1,1024]{2,1,0:T(1,128)} %broadcast_in_dim.35), calls=%async_computation.4 | async-start | bytes 524288 | tf_op jit(solution)/shard_map/all_to_all | solution.py:20
  152.0 84.4 %reduce-scatter.2.cloned.1.call-start = ((), (), s32[]{:S(2)}) async-start(), calls=%async_computation.11 | async-start | bytes 2359296 | tf_op jit(solution)/shard_map/reduce_scatter | solution.py:72
  164.2 14.7 %copy-start.2 = (f32[1024,512]{1,0:T(8,128)S(1)}, f32[1024,512]{1,0:T(8,128)}, u32[]{:S(2)}) copy-start(f32[1024,512]{1,0:T(8,128)} %all-gather.2.cloned.1.call-done) | copy-start | bytes 6291460
  167.9 10.9 %all-to-all-start.5 = ((f32[8,1,1024]{2,1,0:T(1,128)}), f32[8,1,1024]{2,1,0:T(1,128)S(1)}, u32[]{:S(2)}, u32[]{:S(2)}) async-start(f32[8,1,1024]{2,1,0:T(1,128)} %broadcast_in_dim.36), calls=%async_computation.5 | async-start | bytes 65536 | tf_op jit(solution)/shard_map/all_to_all | solution.py:20
  184.9 1.3 copy-start.4
  186.3 6.1 %collective-permute-start = (f32[32,8,1024]{2,1,0:T(8,128)S(1)}, f32[32,8,1024]{2,1,0:T(8,128)S(1)}, u32[]{:S(2)}, u32[]{:S(2)}) collective-permute-start(f32[32,8,1024]{2,1,0:T(8,128)S(1)} %dynamic-slice_bitcast_fusion), channel_id=1, source_target_pairs={{0,8},{8,0},{1,9},{9,1},{2,10},{10,2},{3,11},{11,3},{4,12},{12,4},... | collective-permute-start | bytes 3145736 | tf_op jit(solution)/shard_map/ppermute | solution.py:63
  194.8 18.4 %all-to-all-start.6 = ((f32[4,8,8,1024]{3,2,1,0:T(8,128)}), f32[4,8,8,1024]{3,2,1,0:T(8,128)S(1)}, u32[]{:S(2)}, u32[]{:S(2)}) async-start(f32[4,8,8,1024]{3,2,1,0:T(8,128)} %bitcast.3), calls=%async_computation.6 | async-start | bytes 2097152 | tf_op jit(solution)/shard_map/all_to_all | solution.py:24
  201.5 35.0 %copy-start.5 = (f32[128,512]{1,0:T(8,128)S(1)}, f32[128,512]{1,0:T(8,128)}, u32[]{:S(2)}) copy-start(f32[128,512]{1,0:T(8,128)} %param.3) | copy-start | bytes 786436
  214.1 18.5 %all-to-all-start.8 = ((f32[64,1,1024]{2,1,0:T(1,128)}), f32[64,1,1024]{2,1,0:T(1,128)S(1)}, u32[]{:S(2)}, u32[]{:S(2)}) async-start(f32[64,1,1024]{2,1,0:T(1,128)} %broadcast_in_dim.37), calls=%async_computation.8 | async-start | bytes 524288 | tf_op jit(solution)/shard_map/all_to_all | solution.py:20
  232.5 14.8 %all-to-all-start.7 = ((f32[8,8,1024]{2,1,0:T(8,128)}), f32[8,8,1024]{2,1,0:T(8,128)S(1)}, u32[]{:S(2)}, u32[]{:S(2)}) async-start(f32[8,8,1024]{2,1,0:T(8,128)} %reduce_sum.176), calls=%async_computation.7 | async-start | bytes 524288 | tf_op jit(solution)/shard_map/all_to_all | solution.py:24
Sparse Core Ops, SparseCore 0:
  10.1 46.0 all-gather.1
  155.7 39.9 reduce-scatter.1
where the time goes:
time: 256 us; the launch traced here: 255 us
  waiting for transfers between devices  112 us (44%)
  starting transfers between devices  39.9 us (16%)
  blocking collectives  36.8 us (14%)
  other arithmetic  29.7 us (12%)
  between operations  14.3 us (6%)
  matrix products  11.6 us (5%)
  local copies, waits for them, and re-layouts  10.5 us (4%)
    all_gather x1, waiting for transfers between devices, body(): gathered = lax.all_gather(items, 'code', axis=0, tiled=True)  46.3 us
    all_to_all x5, waiting for transfers between devices, exchange_sum(): return jnp.sum(lax.all_to_all(copies, axes, 0, 0), axis=0)  42.1 us
    all_to_all x2, blocking collectives, exchange_sum(): return jnp.sum(lax.all_to_all(copies, axes, 0, 0), axis=0)  36.8 us
    all_to_all x5, starting transfers between devices, exchange_sum(): return jnp.sum(lax.all_to_all(copies, axes, 0, 0), axis=0)  28.3 us
    all_to_all x2, waiting for transfers between devices, scatter_sum(): return jnp.sum(lax.all_to_all(blocks, axis, 0, 0), axis=0)  20.8 us
    reduce_sum x3, other arithmetic, body(): row_part = jnp.sum(kernel_vals * col_scale[None, :], axis=1)  8.8 us
    reduce_sum x3, other arithmetic, body(): col_part = jnp.sum(kernel_vals * row_scale[:, None], axis=0)  8.49 us
    all_to_all x2, starting transfers between devices, scatter_sum(): return jnp.sum(lax.all_to_all(blocks, axis, 0, 0), axis=0)  7.73 us
  transfers between devices with their start and end apart: 10, of which 9 were waited for; matrix products, arithmetic and copies ran while one was open for 11% of the time, Pallas kernels for 0%

commit v1 on v0

--- a/solution.py
+++ b/solution.py
@@ -31,7 +31,9 @@
     own_rows, width = items.shape
     total_items = own_rows * code_count * dp_count
     scaled = unit_rows(codewords) * (inverse_temp / width)
-    gathered = lax.all_gather(items, "code", axis=0, tiled=True)
+    gathered = jnp.concatenate(
+        lax.all_to_all(jnp.stack([items] * lax.axis_size("code")), "code", 0, 0), axis=0
+    )
     logits = lax.dot_general(
         unit_rows(gathered),
         scaled,

time: 256 us -> 271 us (1.059)
  blocking collectives: 36.8 us -> 63.1 us
  waiting for transfers between devices: 112 us -> 94.2 us
  local copies, waits for them, and re-layouts: 10.5 us -> 16 us
    all_to_all x0 -> x1, waiting for transfers between devices: none -> 48.3 us  [body(): lax.all_to_all(jnp.stack([items] * lax.axis_size('code')), 'code', 0, 0)]
    all_gather x1 -> x0, waiting for transfers between devices: 46.3 us -> none  [body(): gathered = lax.all_gather(items, 'code', axis=0, tiled=True)]
    all_to_all x2 -> x4, blocking collectives: 36.8 us -> 63.1 us  [exchange_sum(): return jnp.sum(lax.all_to_all(copies, axes, 0, 0), axis=0)]
    all_to_all x5 -> x3, waiting for transfers between devices: 42.1 us -> 22.8 us  [exchange_sum(): return jnp.sum(lax.all_to_all(copies, axes, 0, 0), axis=0)]
    all_to_all x5 -> x3, starting transfers between devices: 28.3 us -> 17 us  [exchange_sum(): return jnp.sum(lax.all_to_all(copies, axes, 0, 0), axis=0)]
    all_to_all x0 -> x1, starting transfers between devices: none -> 11 us  [body(): lax.all_to_all(jnp.stack([items] * lax.axis_size('code')), 'code', 0, 0)]
    mul x0 -> x2, other arithmetic: none -> 3.34 us  [the longest x1 1.79 us: unit_rows(): values * lax.rsqrt(jnp.mean(values * values, axis=-1, keepdims=True) + ep...]
    dot_general x0 -> x1, local copies, waits for them, and re-layouts: none -> 2.95 us  [body(): lax.dot_general(row_scale[:, None] * gathered, kernel_vals, (((0,), (0,))...]
  transfers between devices with their start and end apart: 10 -> 8, of which waited for: 9 -> 7; matrix products, arithmetic and copies ran while one was open for 11% -> 10% of each run, Pallas kernels for 0% -> 0%
where the time goes in v1:
time: 271 us; the launch traced here: 270 us
  waiting for transfers between devices  94.2 us (35%)
  blocking collectives  63.1 us (23%)
  starting transfers between devices  39.4 us (15%)
  other arithmetic  30.9 us (11%)
  local copies, waits for them, and re-layouts  16 us (6%)
  between operations  14.3 us (5%)
  matrix products  11.9 us (4%)
    all_to_all x4, blocking collectives, exchange_sum(): return jnp.sum(lax.all_to_all(copies, axes, 0, 0), axis=0)  63.1 us
    all_to_all x1, waiting for transfers between devices, body(): lax.all_to_all(jnp.stack([items] * lax.axis_size('code')), 'code', 0, 0)  48.3 us
    all_to_all x3, waiting for transfers between devices, exchange_sum(): return jnp.sum(lax.all_to_all(copies, axes, 0, 0), axis=0)  22.8 us
    all_to_all x2, waiting for transfers between devices, scatter_sum(): return jnp.sum(lax.all_to_all(blocks, axis, 0, 0), axis=0)  20.7 us
    all_to_all x3, starting transfers between devices, exchange_sum(): return jnp.sum(lax.all_to_all(copies, axes, 0, 0), axis=0)  17 us
    all_to_all x1, starting transfers between devices, body(): lax.all_to_all(jnp.stack([items] * lax.axis_size('code')), 'code', 0, 0)  11 us
    reduce_sum x3, other arithmetic, body(): row_part = jnp.sum(kernel_vals * col_scale[None, :], axis=1)  8.79 us
    reduce_sum x3, other arithmetic, body(): col_part = jnp.sum(kernel_vals * row_scale[:, None], axis=0)  8.41 us
  transfers between devices with their start and end apart: 8, of which 7 were waited for; matrix products, arithmetic and copies ran while one was open for 10% of the time, Pallas kernels for 0%

profile of v1, /device:TPU:1, one launch (start us, length us, event | category | flops | bytes accessed | tf_op | source)
XLA Modules:
  0.0 269.8 jit_solution(4308165803321121156)
XLA Ops:
  7.2 1.1 copy.16
  8.2 1.4 stack.2
  9.7 11.0 %all-to-all-start = ((f32[8,128,512]{1,2,0:T(8,128)}), f32[8,128,512]{1,2,0:T(8,128)}, u32[]{:S(2)}, u32[]{:S(2)}) async-start(f32[8,128,512]{1,2,0:T(8,128)} %stack.2), calls=%async_computation | async-start | bytes 4194304 | tf_op jit(solution)/shard_map/all_to_all | solution.py:35
  20.7 0.2 multiply_reduce_fusion.6
  20.9 48.3 %all-to-all-done = f32[8,128,512]{1,2,0:T(8,128)} async-done(((f32[8,128,512]{1,2,0:T(8,128)}), f32[8,128,512]{1,2,0:T(8,128)}, u32[]{:S(2)}, u32[]{:S(2)}) %all-to-all-start) | async-done | bytes 2097184 | tf_op jit(solution)/shard_map/all_to_all | solution.py:35
  69.2 1.7 multiply_reduce_fusion.7
  70.9 2.9 %copy.17 = f32[8,128,512]{2,1,0:T(8,128)} copy(f32[8,128,512]{1,2,0:T(8,128)} %all-to-all-done) | data formatting | bytes 4194304 | tf_op jit(solution)/shard_map/all_to_all | solution.py:35
  73.9 1.8 bitcast_multiply_fusion.1
  75.7 5.6 %exponential_reduce_fusion = (f32[1024]{0:T(1024)S(1)}, f32[1024,1024]{1,0:T(8,128)}) fusion(f32[1024,512]{1,0:T(8,128)S(1)} %bitcast_multiply_fusion.1, f32[1024,512]{1,0:T(8,128)S(1)} %copy-done, f32[1024]{0:T(1024)S(1)} %add_rsqrt_fusion), kind=kOutput, calls=%fused_computation.10 | convolution fusion | flops 3223321600 | bytes 8396800 | tf_op jit(solution)/shard_map/dot_general | solution.py:37
  81.4 25.7 %all_to_all.57 = f32[64,1,1024]{2,1,0:T(1,128)S(1)} all-to-all(f32[64,1,1024]{2,1,0:T(1,128)S(1)} %broadcast_in_dim.31), channel_id=1, replica_groups=mesh['x'=4,'y'=8,'core'=2,'code'=8] {'x','y','core'}, dimensions={0} | all-to-all | bytes 524288 | tf_op jit(solution)/shard_map/all_to_all | solution.py:20
  107.1 0.2 reduce_sum.165
  107.3 2.9 %multiply_reduce_fusion.5 = f32[1024]{0:T(1024)S(1)} fusion(f32[1024,1024]{1,0:T(8,128)} %get-tuple-element.5, f32[1024]{0:T(1024)S(1)} %multiply_divide_fusion.5), kind=kLoop, calls=%fused_computation.8 | loop fusion | flops 2096128 | bytes 4202496 | tf_op jit(solution)/shard_map/reduce_sum | solution.py:48
  110.2 9.2 %all_to_all.58 = f32[8,1,1024]{2,1,0:T(1,128)S(1)} all-to-all(f32[8,1,1024]{2,1,0:T(1,128)S(1)} %broadcast_in_dim.32), channel_id=1, replica_groups=mesh['x'=4,'y'=8,'core'=2,'code'=8] {'code'}, dimensions={0} | all-to-all | bytes 65536 | tf_op jit(solution)/shard_map/all_to_all | solution.py:20
  119.5 2.8 %multiply_reduce_fusion.4 = f32[1024]{0:T(1024)S(1)} fusion(f32[1024,1024]{1,0:T(8,128)} %get-tuple-element.5, f32[1024]{0:T(1024)S(1)} %multiply_divide_fusion.4), kind=kLoop, calls=%fused_computation.7 | loop fusion | flops 2096128 | bytes 4202496 | tf_op jit(solution)/shard_map/reduce_sum | solution.py:50
  122.4 19.0 %all_to_all.59 = f32[64,1,1024]{2,1,0:T(1,128)S(1)} all-to-all(f32[64,1,1024]{2,1,0:T(1,128)S(1)} %broadcast_in_dim.33), channel_id=1, replica_groups=mesh['x'=4,'y'=8,'core'=2,'code'=8] {'x','y','core'}, dimensions={0} | all-to-all | bytes 524288 | tf_op jit(solution)/shard_map/all_to_all | solution.py:20
  141.4 0.2 reduce_sum.169
  141.5 2.9 %multiply_reduce_fusion.3 = f32[1024]{0:T(1024)S(1)} fusion(f32[1024,1024]{1,0:T(8,128)} %get-tuple-element.5, f32[1024]{0:T(1024)S(1)} %multiply_divide_fusion.3), kind=kLoop, calls=%fused_computation.6 | loop fusion | flops 2096128 | bytes 4202496 | tf_op jit(solution)/shard_map/reduce_sum | solution.py:48
  144.5 9.2 %all_to_all.60 = f32[8,1,1024]{2,1,0:T(1,128)S(1)} all-to-all(f32[8,1,1024]{2,1,0:T(1,128)S(1)} %broadcast_in_dim.34), channel_id=1, replica_groups=mesh['x'=4,'y'=8,'core'=2,'code'=8] {'code'}, dimensions={0} | all-to-all | bytes 65536 | tf_op jit(solution)/shard_map/all_to_all | solution.py:20
  153.8 2.8 %multiply_reduce_fusion.2 = f32[1024]{0:T(1024)S(1)} fusion(f32[1024,1024]{1,0:T(8,128)} %get-tuple-element.5, f32[1024]{0:T(1024)S(1)} %multiply_divide_fusion.2), kind=kLoop, calls=%fused_computation.5 | loop fusion | flops 2096128 | bytes 4202496 | tf_op jit(solution)/shard_map/reduce_sum | solution.py:50
  156.5 0.8 broadcast_in_dim.35
  157.4 7.2 %all-to-all-start.5 = ((f32[64,1,1024]{2,1,0:T(1,128)}), f32[64,1,1024]{2,1,0:T(1,128)S(1)}, u32[]{:S(2)}, u32[]{:S(2)}) async-start(f32[64,1,1024]{2,1,0:T(1,128)} %broadcast_in_dim.35), calls=%async_computation.5 | async-start | bytes 524288 | tf_op jit(solution)/shard_map/all_to_all | solution.py:20
  164.6 4.9 %gather_fusion = f32[1024,512]{1,0:T(8,128)} fusion(f32[1024,512]{1,0:T(8,128)S(1)} %copy-done, s32[1024]{0:T(1024)S(1)} %fusion.8), kind=kCustom, calls=%fused_computation | custom fusion | bytes 4198400 | tf_op jit(solution)/shard_map/jit(_take)/gather | solution.py:73
  169.5 7.1 %all-to-all-done.5 = f32[64,1,1024]{2,1,0:T(1,128)S(1)} async-done(((f32[64,1,1024]{2,1,0:T(1,128)}), f32[64,1,1024]{2,1,0:T(1,128)S(1)}, u32[]{:S(2)}, u32[]{:S(2)}) %all-to-all-start.5) | async-done | bytes 262176 | tf_op jit(solution)/shard_map/all_to_all | solution.py:20
  176.6 0.2 reduce_sum.173
  176.8 3.0 %multiply_reduce_fusion.1 = f32[1024]{0:T(1024)S(1)} fusion(f32[1024,1024]{1,0:T(8,128)} %get-tuple-element.5, f32[1024]{0:T(1024)S(1)} %multiply_divide_fusion.1), kind=kLoop, calls=%fused_computation.4 | loop fusion | flops 2096128 | bytes 4202496 | tf_op jit(solution)/shard_map/reduce_sum | solution.py:48
  179.8 0.6 broadcast_in_dim.36
  180.4 3.3 %all-to-all-start.6 = ((f32[8,1,1024]{2,1,0:T(1,128)}), f32[8,1,1024]{2,1,0:T(1,128)S(1)}, u32[]{:S(2)}, u32[]{:S(2)}) async-start(f32[8,1,1024]{2,1,0:T(1,128)} %broadcast_in_dim.36), calls=%async_computation.6 | async-start | bytes 65536 | tf_op jit(solution)/shard_map/all_to_all | solution.py:20
  183.8 0.2 reduce-scatter.2.cloned.1.call-start
  184.0 2.0 select_select_fusion
  186.0 4.5 %all-to-all-done.6 = f32[8,1,1024]{2,1,0:T(1,128)S(1)} async-done(((f32[8,1,1024]{2,1,0:T(1,128)}), f32[8,1,1024]{2,1,0:T(1,128)S(1)}, u32[]{:S(2)}, u32[]{:S(2)}) %all-to-all-start.6) | async-done | bytes 32800 | tf_op jit(solution)/shard_map/all_to_all | solution.py:20
  190.6 1.5 bitcast_multiply_fusion
  192.2 3.0 %copy.24 = f32[512,1024]{1,0:T(8,128)} copy(f32[512,1024]{0,1:T(8,128)} %bitcast.22) | data formatting | bytes 4194304 | tf_op jit(solution)/shard_map/dot_general | solution.py:54
  195.1 6.3 %fusion = f32[32,2,8,1024]{3,2,1,0:T(8,128)S(1)} fusion(f32[32,2,8,1024]{3,2,1,0:T(8,128)} %bitcast.21, f32[1024,1024]{1,0:T(8,128)} %get-tuple-element.5), kind=kOutput, calls=%fused_computation.1 | convolution fusion | flops 3221225472 | bytes 8388608 | tf_op jit(solution)/shard_map/dot_general | solution.py:54
  201.6 3.5 %collective-permute-start = (f32[32,8,1024]{2,1,0:T(8,128)S(1)}, f32[32,8,1024]{2,1,0:T(8,128)}, u32[]{:S(2)}, u32[]{:S(2)}) collective-permute-start(f32[32,8,1024]{2,1,0:T(8,128)S(1)} %dynamic-slice_bitcast_fusion), channel_id=1, source_target_pairs={{0,8},{8,0},{1,9},{9,1},{2,10},{10,2},{3,11},{11,3},{4,12},{12,4},... | collective-permute-start | bytes 3145736 | tf_op jit(solution)/shard_map/ppermute | solution.py:65
  205.1 2.4 collective-permute-done
  207.5 2.4 bitcast_add_fusion
  209.9 3.7 %all-to-all-start.7 = ((f32[4,8,8,1024]{3,2,1,0:T(8,128)}), f32[4,8,8,1024]{3,2,1,0:T(8,128)S(1)}, u32[]{:S(2)}, u32[]{:S(2)}) async-start(f32[4,8,8,1024]{3,2,1,0:T(8,128)} %bitcast.8), calls=%async_computation.7 | async-start | bytes 2097152 | tf_op jit(solution)/shard_map/all_to_all | solution.py:24
  213.6 2.8 %multiply_reduce_fusion = f32[1024]{0:T(1024)S(1)} fusion(f32[1024,1024]{1,0:T(8,128)} %get-tuple-element.5, f32[1024]{0:T(1024)S(1)} %multiply_divide_fusion), kind=kLoop, calls=%fused_computation.3 | loop fusion | flops 2096128 | bytes 4202496 | tf_op jit(solution)/shard_map/reduce_sum | solution.py:50
  216.5 11.7 %all-to-all-done.7 = f32[4,8,8,1024]{3,2,1,0:T(8,128)S(1)} async-done(((f32[4,8,8,1024]{3,2,1,0:T(8,128)}), f32[4,8,8,1024]{3,2,1,0:T(8,128)S(1)}, u32[]{:S(2)}, u32[]{:S(2)}) %all-to-all-start.7) | async-done | bytes 1048608 | tf_op jit(solution)/shard_map/all_to_all | solution.py:24
  228.2 0.8 broadcast_in_dim.37
  229.0 6.5 %all-to-all-start.9 = ((f32[64,1,1024]{2,1,0:T(1,128)}), f32[64,1,1024]{2,1,0:T(1,128)S(1)}, u32[]{:S(2)}, u32[]{:S(2)}) async-start(f32[64,1,1024]{2,1,0:T(1,128)} %broadcast_in_dim.37), calls=%async_computation.9 | async-start | bytes 524288 | tf_op jit(solution)/shard_map/all_to_all | solution.py:20
  235.5 0.8 reduce_sum.176
  236.3 11.2 %all-to-all-done.9 = f32[64,1,1024]{2,1,0:T(1,128)S(1)} async-done(((f32[64,1,1024]{2,1,0:T(1,128)}), f32[64,1,1024]{2,1,0:T(1,128)S(1)}, u32[]{:S(2)}, u32[]{:S(2)}) %all-to-all-start.9) | async-done | bytes 262176 | tf_op jit(solution)/shard_map/all_to_all | solution.py:20
  247.5 3.9 %all-to-all-start.8 = ((f32[8,8,1024]{2,1,0:T(8,128)}), f32[8,8,1024]{2,1,0:T(8,128)S(1)}, u32[]{:S(2)}, u32[]{:S(2)}) async-start(f32[8,8,1024]{2,1,0:T(8,128)} %reduce_sum.176), calls=%async_computation.8 | async-start | bytes 524288 | tf_op jit(solution)/shard_map/all_to_all | solution.py:24
  251.4 1.7 sub.15
  253.1 0.2 reduce_sum.179
  253.3 9.0 %all-to-all-done.8 = f32[8,8,1024]{2,1,0:T(8,128)S(1)} async-done(((f32[8,8,1024]{2,1,0:T(8,128)}), f32[8,8,1024]{2,1,0:T(8,128)S(1)}, u32[]{:S(2)}, u32[]{:S(2)}) %all-to-all-start.8) | async-done | bytes 262176 | tf_op jit(solution)/shard_map/all_to_all | solution.py:24
  262.4 0.6 divide_bitcast_fusion
  (31 shorter events, 0.7 us)
Async XLA Ops:
  9.7 11.0 %copy-start = (f32[1024,512]{1,0:T(8,128)S(1)}, f32[1024,512]{1,0:T(8,128)}, u32[]{:S(2)}) copy-start(f32[1024,512]{1,0:T(8,128)} %param.4) | copy-start | bytes 6291460
  9.7 59.5 %all-to-all-start = ((f32[8,128,512]{1,2,0:T(8,128)}), f32[8,128,512]{1,2,0:T(8,128)}, u32[]{:S(2)}, u32[]{:S(2)}) async-start(f32[8,128,512]{1,2,0:T(8,128)} %stack.2), calls=%async_computation | async-start | bytes 4194304 | tf_op jit(solution)/shard_map/all_to_all | solution.py:35
  153.7 10.8 %copy-start.4 = (s32[1024]{0:T(1024)S(1)}, s32[1024]{0:T(1024)}, u32[]{:S(2)}) copy-start(s32[1024]{0:T(1024)} %param.5) | copy-start | bytes 12292
  157.4 19.2 %all-to-all-start.5 = ((f32[64,1,1024]{2,1,0:T(1,128)}), f32[64,1,1024]{2,1,0:T(1,128)S(1)}, u32[]{:S(2)}, u32[]{:S(2)}) async-start(f32[64,1,1024]{2,1,0:T(1,128)} %broadcast_in_dim.35), calls=%async_computation.5 | async-start | bytes 524288 | tf_op jit(solution)/shard_map/all_to_all | solution.py:20
  176.8 7.3 %copy-start.2 = (f32[1024,512]{1,0:T(8,128)S(1)}, f32[1024,512]{1,0:T(8,128)}, u32[]{:S(2)}) copy-start(f32[1024,512]{1,0:T(8,128)} %gather_fusion) | copy-start | bytes 6291460
  180.4 10.1 %all-to-all-start.6 = ((f32[8,1,1024]{2,1,0:T(1,128)}), f32[8,1,1024]{2,1,0:T(1,128)S(1)}, u32[]{:S(2)}, u32[]{:S(2)}) async-start(f32[8,1,1024]{2,1,0:T(1,128)} %broadcast_in_dim.36), calls=%async_computation.6 | async-start | bytes 65536 | tf_op jit(solution)/shard_map/all_to_all | solution.py:20
  183.8 67.6 %reduce-scatter.2.cloned.1.call-start = ((), (), s32[]{:S(2)}) async-start(), calls=%async_computation.11 | async-start | bytes 2359296 | tf_op jit(solution)/shard_map/reduce_scatter | solution.py:74
  186.0 4.6 %copy-start.1 = (f32[8,128,512]{2,1,0:T(8,128)S(1)}, f32[8,128,512]{2,1,0:T(8,128)}, u32[]{:S(2)}) copy-start(f32[8,128,512]{2,1,0:T(8,128)} %copy.17) | copy-start | bytes 6291460
  201.6 5.9 %collective-permute-start = (f32[32,8,1024]{2,1,0:T(8,128)S(1)}, f32[32,8,1024]{2,1,0:T(8,128)}, u32[]{:S(2)}, u32[]{:S(2)}) collective-permute-start(f32[32,8,1024]{2,1,0:T(8,128)S(1)} %dynamic-slice_bitcast_fusion), channel_id=1, source_target_pairs={{0,8},{8,0},{1,9},{9,1},{2,10},{10,2},{3,11},{11,3},{4,12},{12,4},... | collective-permute-start | bytes 3145736 | tf_op jit(solution)/shard_map/ppermute | solution.py:65
  209.9 18.3 %all-to-all-start.7 = ((f32[4,8,8,1024]{3,2,1,0:T(8,128)}), f32[4,8,8,1024]{3,2,1,0:T(8,128)S(1)}, u32[]{:S(2)}, u32[]{:S(2)}) async-start(f32[4,8,8,1024]{3,2,1,0:T(8,128)} %bitcast.8), calls=%async_computation.7 | async-start | bytes 2097152 | tf_op jit(solution)/shard_map/all_to_all | solution.py:24
  216.5 34.9 %copy-start.3 = (f32[128,512]{1,0:T(8,128)S(1)}, f32[128,512]{1,0:T(8,128)}, u32[]{:S(2)}) copy-start(f32[128,512]{1,0:T(8,128)} %param.3) | copy-start | bytes 786436
  229.0 18.5 %all-to-all-start.9 = ((f32[64,1,1024]{2,1,0:T(1,128)}), f32[64,1,1024]{2,1,0:T(1,128)S(1)}, u32[]{:S(2)}, u32[]{:S(2)}) async-start(f32[64,1,1024]{2,1,0:T(1,128)} %broadcast_in_dim.37), calls=%async_computation.9 | async-start | bytes 524288 | tf_op jit(solution)/shard_map/all_to_all | solution.py:20
  247.5 14.8 %all-to-all-start.8 = ((f32[8,8,1024]{2,1,0:T(8,128)}), f32[8,8,1024]{2,1,0:T(8,128)S(1)}, u32[]{:S(2)}, u32[]{:S(2)}) async-start(f32[8,8,1024]{2,1,0:T(8,128)} %reduce_sum.176), calls=%async_computation.8 | async-start | bytes 524288 | tf_op jit(solution)/shard_map/all_to_all | solution.py:24
Sparse Core Ops, SparseCore 0:
  187.5 37.9 reduce-scatter.1
